TPU v7x, 32 devices: a whole 2x2x4 slice. The times are simulated.
32 devices in a mesh: dp: 8 (over y, x, core), vocab: 4 (over z).
Axes of the slice: x: 2, y: 2, z: 4, core: 2. Of those that a mesh axis runs over, the one named last changes fastest.
Arguments:
- hidden: bfloat16 [384, 8192], P('dp', 'vocab'), may hold values from -32 to 32
- head_weight: bfloat16 [8192, 128256], P(None, ('dp', 'vocab')), may hold values from -0.9943689 to 0.9943689
- critic_in: bfloat16 [8, 8192, 4096], P('dp', None, 'vocab'), may hold values from -0.0625 to 0.0625
- critic_out: bfloat16 [8, 4096], P('dp', 'vocab'), may hold values from -0.09375 to 0.09375
- rewards: float32 [8, 12], P('dp'), may hold values from -4 to 4
- turn_ids: int32 [8, 48], P('dp'), may hold values from 0 to 11, never falling along the last dimension, each value on 1 to 8 neighbouring positions
- owners: int32 [96, 1], P('dp'), may hold values from 0 to 7; in each aligned block of 12 rows (0 to 11, 12 to 23, ...) at most 3 rows name the same one
- actions: int32 [384], replicated, may hold values from 0 to 128255
Outputs:
- hidden_grad: float32 [384, 8192], P('dp', 'vocab')
- token_logprob: float32 [384], P('dp')
- turn_advantage: float32 [8, 12], P('dp')
Inputs may be any that keep to these rules, and one draw needn't show every extreme that they name: `turn_ids`: in each row, turn numbers never fall, every number of 0 to 11 appears, and each turn has 1 to 8 tokens. `owners`: among the 12 turns of one index of dp, at most 3 name the same critic, and every critic is named by some turn.
All inputs are finite; a program needn't handle non-finite values.
Results may differ from a plain program's by a relative error of at most 0.0087.
Values may be sent and summed in bfloat16 or wider, within the bound.
A program may use at most 192 MiB of HBM per device.

v0:
```python
import functools

import jax
import jax.numpy as jnp
from jax import lax
from jax.experimental import pallas as pl
from jax.experimental.pallas import tpu as pltpu
from jax.sharding import PartitionSpec as P


epsilon = 1e-05
loss_scale = 32.0
MESH = pl.DeviceIdType.MESH


def rms_norm(values):
    return values * lax.rsqrt(jnp.mean(values * values, axis=-1, keepdims=True) + epsilon)


def exchange_kernel(ranks_dp, ranks_vocab, over_vocab, block_ref, all_ref, send_sem, recv_sem, own_sem):
    my_dp, my_vocab = lax.axis_index("dp"), lax.axis_index("vocab")
    count = ranks_dp * ranks_vocab if over_vocab else ranks_dp
    me = my_dp * ranks_vocab + my_vocab if over_vocab else my_dp

    def place(step):
        peer = lax.rem(me + step, count)
        if over_vocab:
            return (lax.div(peer, ranks_vocab), lax.rem(peer, ranks_vocab))
        return (peer, my_vocab)

    barrier = pltpu.get_barrier_semaphore()
    for step in range(1, count):
        pl.semaphore_signal(barrier, inc=1, device_id=place(step), device_id_type=MESH)
    pl.semaphore_wait(barrier, count - 1)
    own = pltpu.make_async_copy(block_ref, all_ref.at[me], own_sem)
    own.start()
    copies = []
    for step in range(1, count):
        copy = pltpu.make_async_remote_copy(
            src_ref=block_ref,
            dst_ref=all_ref.at[me],
            send_sem=send_sem.at[step],
            recv_sem=recv_sem.at[step],
            device_id=place(step),
            device_id_type=MESH,
        )
        copy.start()
        copies.append(copy)
    own.wait()
    for copy in copies:
        copy.wait()


def exchange(block, over_vocab, collective_id):
    ranks_dp, ranks_vocab = lax.axis_size("dp"), lax.axis_size("vocab")
    count = ranks_dp * ranks_vocab if over_vocab else ranks_dp
    return pl.pallas_call(
        functools.partial(exchange_kernel, ranks_dp, ranks_vocab, over_vocab),
        out_shape=jax.ShapeDtypeStruct((count,) + block.shape, block.dtype),
        in_specs=[pl.BlockSpec(memory_space=pltpu.VMEM)],
        out_specs=pl.BlockSpec(memory_space=pltpu.VMEM),
        scratch_shapes=[
            pltpu.SemaphoreType.DMA((count,)),
            pltpu.SemaphoreType.DMA((count,)),
            pltpu.SemaphoreType.DMA,
        ],
        compiler_params=pltpu.CompilerParams(collective_id=collective_id, has_side_effects=True),
    )(block)


def gather_kernel(
    ranks_dp, ranks_vocab, x_ref, facts_ref, all_ref, facts_all_ref,
    own_sem, facts_send, facts_recv, side_send, side_recv, send_sem, recv_sem,
):
    me, col = lax.axis_index("dp"), lax.axis_index("vocab")
    width = x_ref.shape[1]
    half = width // 2
    bits = list(range(1, ranks_dp.bit_length() - 1))
    orders = (bits + [0], bits[::-1] + [0])
    rounds = len(orders[0])

    barrier = pltpu.get_barrier_semaphore()
    for step in range(1, ranks_dp):
        pl.semaphore_signal(barrier, inc=1, device_id=(me ^ step, col), device_id_type=MESH)
    for step in range(1, ranks_vocab):
        pl.semaphore_signal(barrier, inc=1, device_id=(me, col ^ step), device_id_type=MESH)
    pl.semaphore_wait(barrier, ranks_dp + ranks_vocab - 2)

    mine = all_ref.at[me, :, pl.ds(pl.multiple_of(col * width, 128), width)]
    own = [
        pltpu.make_async_copy(x_ref, mine, own_sem.at[0]),
        pltpu.make_async_copy(facts_ref, facts_all_ref.at[me], own_sem.at[1]),
    ]
    for copy in own:
        copy.start()
    side = {}
    for step in range(1, ranks_vocab):
        side[step] = pltpu.make_async_remote_copy(
            src_ref=x_ref, dst_ref=mine,
            send_sem=side_send.at[step], recv_sem=side_recv.at[step],
            device_id=(me, col ^ step), device_id_type=MESH,
        )
        side[step].start()
    others = []
    for step in range(1, ranks_dp):
        copy = pltpu.make_async_remote_copy(
            src_ref=facts_ref, dst_ref=facts_all_ref.at[me],
            send_sem=facts_send.at[step], recv_sem=facts_recv.at[step],
            device_id=(me ^ step, col), device_id_type=MESH,
        )
        copy.start()
        others.append(copy)
    for copy in own:
        copy.wait()

    moves = {}
    for time in range(ranks_vocab + rounds - 1):
        for turn in range(rounds - 1, -1, -1):
            piece = time - turn
            if not 0 <= piece < ranks_vocab:
                continue
            if turn == 0 and piece > 0:
                side[piece].wait_recv()
            for part in (0, 1):
                order = orders[part]
                if turn > 0:
                    for copy in moves[piece, part, turn - 1]:
                        copy.wait_recv()
                start = pl.multiple_of((col ^ piece) * width + part * half, 128)
                started = []
                for k in range(1 << turn):
                    mask = sum(1 << order[i] for i in range(turn) if k >> i & 1)
                    block = all_ref.at[me ^ mask, :, pl.ds(start, half)]
                    slot = (1 << turn) + k
                    copy = pltpu.make_async_remote_copy(
                        src_ref=block, dst_ref=block,
                        send_sem=send_sem.at[piece, part, slot],
                        recv_sem=recv_sem.at[piece, part, slot],
                        device_id=(me ^ (1 << order[turn]), col), device_id_type=MESH,
                    )
                    copy.start()
                    started.append(copy)
                moves[piece, part, turn] = started
    for (piece, part, turn), started in moves.items():
        for copy in started:
            if turn == rounds - 1:
                copy.wait_recv()
            copy.wait_send()
    for copy in side.values():
        copy.wait_send()
    for copy in others:
        copy.wait()


def gather(x, facts):
    ranks_dp, ranks_vocab = lax.axis_size("dp"), lax.axis_size("vocab")
    dma = pltpu.SemaphoreType.DMA
    everything, facts_all = pl.pallas_call(
        functools.partial(gather_kernel, ranks_dp, ranks_vocab),
        out_shape=(
            jax.ShapeDtypeStruct((ranks_dp, x.shape[0], x.shape[1] * ranks_vocab), x.dtype),
            jax.ShapeDtypeStruct((ranks_dp,) + facts.shape, facts.dtype),
        ),
        in_specs=[pl.BlockSpec(memory_space=pltpu.VMEM)] * 2,
        out_specs=[pl.BlockSpec(memory_space=pltpu.VMEM)] * 2,
        scratch_shapes=[
            dma((2,)),
            dma((ranks_dp,)),
            dma((ranks_dp,)),
            dma((ranks_vocab,)),
            dma((ranks_vocab,)),
            dma((ranks_vocab, 2, ranks_dp)),
            dma((ranks_vocab, 2, ranks_dp)),
        ],
        compiler_params=pltpu.CompilerParams(collective_id=1, has_side_effects=True),
    )(x, facts)
    return everything.reshape(-1, everything.shape[2]), facts_all


def halve(parts, axis_name, bit, axis):
    ranks = lax.axis_size(axis_name)
    mine = (lax.axis_index(axis_name) >> bit) & 1
    first, second = [lax.index_in_dim(parts, i, axis, keepdims=False) for i in (0, 1)]
    kept = jnp.where(mine == 0, first, second)
    sent = jnp.where(mine == 0, second, first)
    got = lax.ppermute(sent, axis_name, [(i, i ^ (1 << bit)) for i in range(ranks)])
    return kept.astype(jnp.float32) + got.astype(jnp.float32)


def advance(chunks, number, orders, step):
    states, order = chunks[number], orders[number % 2]
    if len(states) == step + 1:
        axis = sorted(order[step:], reverse=True).index(order[step])
        states.append(halve(states[-1], "dp", order[step], axis).astype(jnp.bfloat16))
    return states[step + 1]


def on_device(hidden, head_weight, critic_in, critic_out, rewards, turn_ids, owners, actions):
    ranks_dp = lax.axis_size("dp")
    ranks_vocab = lax.axis_size("vocab")
    my_dp, my_vocab = lax.axis_index("dp"), lax.axis_index("vocab")
    tok_dev = hidden.shape[0]
    tokens = tok_dev * ranks_dp
    width = hidden.shape[1]
    turn_dev = rewards.shape[1]
    turns = turn_dev * ranks_dp
    slot_count = max(2, 2 * turn_dev // ranks_dp)
    vocab_local = head_weight.shape[1]

    lanes = -(-max(tok_dev, turn_dev) // 128) * 128

    def row(values):
        return jnp.pad(values.astype(jnp.float32), (0, lanes - values.shape[0]))[None, :]

    facts = jnp.concatenate(
        [row(turn_ids[0]), row(owners[:, 0]), row(rewards[0]), jnp.zeros((5, lanes), jnp.float32)]
    )
    hidden_all, facts = gather(hidden, facts)
    ids_all = facts[:, 0, :tok_dev].astype(jnp.int32)
    owner_all = facts[:, 1, :turn_dev].astype(jnp.int32)
    rewards_all = facts[:, 2, :turn_dev]

    position = jnp.arange(tok_dev, dtype=jnp.int32)
    turn_range = jnp.arange(turn_dev, dtype=jnp.int32)
    member = ids_all[:, None, :] == turn_range[None, :, None]
    last_pos = jnp.max(jnp.where(member, position, -1), axis=2)
    earlier = (owner_all[:, None, :] == owner_all[:, :, None]) & (
        turn_range[None, :] < turn_range[:, None]
    )
    slot_of = jnp.sum(earlier.astype(jnp.int32), axis=2)
    per_critic = ranks_dp * slot_count
    place = (owner_all * ranks_dp + jnp.arange(ranks_dp, dtype=jnp.int32)[:, None]) * slot_count
    place = (place + slot_of).reshape(turns)
    end_token = (jnp.arange(ranks_dp, dtype=jnp.int32)[:, None] * tok_dev + last_pos).reshape(turns)
    slots = my_dp * per_critic + jnp.arange(per_critic, dtype=jnp.int32)
    token_of_slot = jnp.sum(
        jnp.where(place[None, :] == slots[:, None], end_token[None, :] + 1, 0), axis=1
    ) - 1
    pick = (jnp.arange(tokens, dtype=jnp.int32)[None, :] == token_of_slot[:, None]).astype(
        jnp.bfloat16
    )
    place_tok = jnp.sum(
        jnp.where(member, place.reshape(ranks_dp, turn_dev)[:, :, None], 0), axis=1
    ).reshape(tokens)
    reward_tok = jnp.sum(jnp.where(member, rewards_all[:, :, None], 0.0), axis=1).reshape(tokens)
    place_own = lax.dynamic_slice_in_dim(place, my_dp * turn_dev, turn_dev, 0)

    rows = jnp.dot(pick, hidden_all, preferred_element_type=jnp.float32)
    normed = rms_norm(rows).astype(jnp.bfloat16)
    inner = jnp.dot(normed, critic_in[0], preferred_element_type=jnp.float32)
    active = jax.nn.silu(inner).astype(jnp.bfloat16)
    value_part = jnp.sum(
        active.astype(jnp.float32) * critic_out[0].astype(jnp.float32)[None, :], axis=1
    )

    logits = jnp.dot(hidden_all, head_weight, preferred_element_type=jnp.float32)
    first_col = (my_dp * ranks_vocab + my_vocab) * vocab_local
    hit = jnp.arange(vocab_local, dtype=jnp.int32)[None, :] == (actions - first_col)[:, None]
    picked_part = jnp.sum(jnp.where(hit, logits, 0.0), axis=1)
    top_part = jnp.max(logits, axis=1)
    mass_part = jnp.sum(jnp.exp(logits - top_part[:, None]), axis=1)

    stats = jnp.stack(
        [top_part, mass_part, picked_part, jnp.pad(value_part, (0, tokens - per_critic))]
        + [jnp.zeros((tokens,), jnp.float32)] * 4
    )
    stats = exchange(stats, True, 2)
    row_top = jnp.max(stats[:, 0], axis=0)
    row_mass = jnp.sum(stats[:, 1] * jnp.exp(stats[:, 0] - row_top[None, :]), axis=0)
    picked = jnp.sum(stats[:, 2], axis=0)
    logprob_all = picked - row_top - jnp.log(row_mass)
    token_logprob = lax.dynamic_slice_in_dim(logprob_all, my_dp * tok_dev, tok_dev, 0)
    values = jnp.sum(
        stats[:, 3, :per_critic].reshape(ranks_dp, ranks_vocab, per_critic), axis=1
    ).reshape(-1)
    all_places = jnp.arange(ranks_dp * per_critic, dtype=jnp.int32)

    def value_at(places):
        return jnp.sum(jnp.where(places[:, None] == all_places[None, :], values[None, :], 0.0), axis=1)

    advantage = rewards[0] - value_at(place_own)
    token_adv = reward_tok - value_at(place_tok)

    probs = jnp.exp(logits - row_top[:, None]) / row_mass[:, None]
    grad_logits = (loss_scale * token_adv[:, None] * (probs - hit.astype(jnp.float32))).astype(
        jnp.bfloat16
    )
    grad_logits = lax.optimization_barrier(grad_logits)

    dp_bits = list(range(ranks_dp.bit_length() - 1))
    orders = (dp_bits, dp_bits[:1] + dp_bits[:0:-1])
    half = width // 2
    chunks = []
    for number in range(2 * ranks_vocab):
        weight = lax.slice_in_dim(head_weight, number * half, (number + 1) * half, axis=0)
        part = lax.dot_general(
            grad_logits, weight, (((1,), (1,)), ((), ())), preferred_element_type=jnp.float32
        ).astype(jnp.bfloat16)
        chunks.append([part.reshape((2,) * len(dp_bits) + (tok_dev, half))])
    for step in range(len(dp_bits)):
        for number in range(2 * ranks_vocab):
            advance(chunks, number, orders, step)
    blocks = [[chunks[2 * i + k][-1] for k in (0, 1)] for i in range(ranks_vocab)]
    bit = 0
    while len(blocks) > 1:
        joined = []
        for i in range(0, len(blocks), 2):
            pair = []
            for k in (0, 1):
                both = jnp.stack([blocks[i][k], blocks[i + 1][k]])
                pair.append(halve(both, "vocab", bit, 0))
            joined.append(pair)
        blocks = joined
        if len(blocks) > 1:
            blocks = [[x.astype(jnp.bfloat16) for x in pair] for pair in blocks]
        bit += 1
    hidden_grad = jnp.concatenate(blocks[0], axis=1)
    return (hidden_grad, token_logprob, advantage[None, :])


def solution(mesh):
    return jax.shard_map(
        on_device,
        mesh=mesh,
        in_specs=(
            P("dp", "vocab"),
            P(None, ("dp", "vocab")),
            P("dp", None, "vocab"),
            P("dp", "vocab"),
            P("dp", None),
            P("dp", None),
            P("dp", None),
            P(),
        ),
        out_specs=(P("dp", "vocab"), P("dp"), P("dp", None)),
        check_vma=False,
    )
```

profile of v0, /device:TPU:0, one launch (start us, length us, event | category | flops | bytes accessed | tf_op | source)
XLA Modules:
  0.0 262.7 jit_solution(5374244834633557423)
XLA Ops:
  3.4 45.7 %shard_map.103 = (bf16[8,48,8192]{2,1,0:T(8,128)(2,1)}, f32[8,8,128]{2,1,0:T(8,128)}) custom-call(bf16[48,2048]{1,0:T(8,128)(2,1)} %x_ref.1, f32[8,128]{1,0:T(8,128)} %maximum_maximum_fusion.facts_ref), custom_call_target="tpu_custom_call" | custom-call | tf_op jit(solution)/shard_map/pallas_call | solution.py:158
  53.0 3.9 %multiply_reduce_fusion = (f32[24]{0:T(128)S(1)}, f32[24,8192]{1,0:T(8,128)S(1)}) fusion(bf16[384,8192]{1,0:T(8,128)(2,1)} %bitcast.233, s32[24]{0:T(128)S(1)} %broadcast_add_fusion), kind=kOutput, calls=%fused_computation.47 | convolution fusion | flops 151397344 | bytes 7078080 | tf_op jit(solution)/shard_map/dot_general | solution.py:248
  56.9 8.3 %multiply_reduce_fusion.1 = f32[24]{0:T(128)S(1)} fusion(bf16[1,8192,1024]{2,1,0:T(8,128)(2,1)} %param.10, f32[24,8192]{1,0:T(8,128)S(1)} %get-tuple-element.46, f32[24]{0:T(128)S(1)} %add_rsqrt_fusion, f32[1024]{0:T(1024)S(1)} %bitcast.253), kind=kOutput, calls=%fused_computation.122 | convolution fusion | flops 403242976 | bytes 17567936 | tf_op jit(solution)/shard_map/dot_general | solution.py:250
  65.2 42.2 %fusion.90 = (f32[384]{0:T(512)S(1)}, f32[384,4008]{0,1:T(8,128)}) fusion(bf16[384,8192]{1,0:T(8,128)(2,1)} %bitcast.234, bf16[8192,4008]{0,1:T(8,128)(2,1)} %param.9), kind=kOutput, calls=%fused_computation.174 | convolution fusion | flops 25217693696 | bytes 78116352 | tf_op jit(solution)/shard_map/dot_general | solution.py:256
  107.4 4.4 %select_reduce_fusion = (f32[384]{0:T(512)S(1)}, f32[384]{0:T(512)S(1)}) fusion(f32[384,4008]{0,1:T(8,128)} %get-tuple-element.44, s32[384]{0:T(512)S(1)} %broadcast_subtract_fusion, f32[384]{0:T(512)S(1)} %get-tuple-element.43), kind=kLoop, calls=%fused_computation.19 | loop fusion | flops 7694592 | bytes 6162432 | tf_op jit(solution)/shard_map/reduce_sum | solution.py:259
  112.5 15.1 %shard_map.104 = f32[32,8,384]{2,1,0:T(8,128)} custom-call(f32[8,384]{1,0:T(8,128)} %stack.23.block_ref), custom_call_target="tpu_custom_call" | custom-call | tf_op jit(solution)/shard_map/pallas_call | solution.py:57
  130.6 4.7 %multiply_convert_fusion = bf16[384,4008]{0,1:T(8,128)(2,1)S(1)} fusion(f32[384,4008]{0,1:T(8,128)} %get-tuple-element.44, f32[384]{0:T(512)S(1)} %fusion.74, f32[384]{0:T(512)S(1)} %get-tuple-element.10, f32[384]{0:T(512)S(1)} %subtract_multiply_fusion, s32[384]{0:T(512)S(1)} %broadcast_subtract_fusion), kind=kLoop, calls=%fused_computation.18 | loop fusion | flops 10773504 | bytes 9240576 | tf_op jit(solution)/shard_map/convert_element_type | solution.py:285
  135.3 7.2 %fusion.27 = bf16[384,1024]{1,0:T(8,128)(2,1)S(1)} fusion(bf16[384,4008]{0,1:T(8,128)(2,1)S(1)} %multiply_convert_fusion, bf16[8192,4008]{0,1:T(8,128)(2,1)} %param.9), kind=kOutput, calls=%fused_computation.25 | convolution fusion | flops 3152412672 | bytes 12072960 | tf_op jit(solution)/shard_map/dot_general | solution.py:296
  143.3 7.8 %fusion.24 = bf16[384,1024]{1,0:T(8,128)(2,1)S(1)} fusion(bf16[384,4008]{0,1:T(8,128)(2,1)} %copy-done.5, bf16[8192,4008]{0,1:T(8,128)(2,1)} %param.9), kind=kOutput, calls=%fused_computation.24 | convolution fusion | flops 3152412672 | bytes 12072960 | tf_op jit(solution)/shard_map/dot_general | solution.py:296
  152.4 6.0 %fusion.21 = bf16[384,1024]{1,0:T(8,128)(2,1)S(1)} fusion(bf16[384,4008]{0,1:T(8,128)(2,1)S(1)} %copy-done.6, bf16[8192,4008]{0,1:T(8,128)(2,1)} %param.9), kind=kOutput, calls=%fused_computation.23 | convolution fusion | flops 3152412672 | bytes 12072960 | tf_op jit(solution)/shard_map/dot_general | solution.py:296
  159.4 6.0 %fusion.18 = bf16[384,1024]{1,0:T(8,128)(2,1)S(1)} fusion(bf16[384,4008]{0,1:T(8,128)(2,1)S(1)} %copy-done.6, bf16[8192,4008]{0,1:T(8,128)(2,1)} %param.9), kind=kOutput, calls=%fused_computation.22 | convolution fusion | flops 3152412672 | bytes 12072960 | tf_op jit(solution)/shard_map/dot_general | solution.py:296
  166.8 6.3 %fusion.39 = bf16[384,1024]{1,0:T(8,128)(2,1)S(1)} fusion(bf16[384,4008]{0,1:T(8,128)(2,1)S(1)} %copy-done.6, bf16[8192,4008]{0,1:T(8,128)(2,1)} %param.9), kind=kOutput, calls=%fused_computation.29 | convolution fusion | flops 3152412672 | bytes 12072960 | tf_op jit(solution)/shard_map/dot_general | solution.py:296
  174.9 8.7 %fusion.36 = bf16[384,1024]{1,0:T(8,128)(2,1)} fusion(bf16[384,4008]{0,1:T(8,128)(2,1)} %copy-done.5, bf16[8192,4008]{0,1:T(8,128)(2,1)} %param.9), kind=kOutput, calls=%fused_computation.28 | convolution fusion | flops 3152412672 | bytes 12072960 | tf_op jit(solution)/shard_map/dot_general | solution.py:296
  183.6 6.9 %fusion.33 = bf16[384,1024]{1,0:T(8,128)(2,1)} fusion(bf16[384,4008]{0,1:T(8,128)(2,1)S(1)} %copy-done.7, bf16[8192,4008]{0,1:T(8,128)(2,1)} %param.9), kind=kOutput, calls=%fused_computation.27 | convolution fusion | flops 3152412672 | bytes 12072960 | tf_op jit(solution)/shard_map/dot_general | solution.py:296
  190.5 6.9 %fusion.30 = bf16[384,1024]{1,0:T(8,128)(2,1)} fusion(bf16[384,4008]{0,1:T(8,128)(2,1)S(1)} %copy-done.7, bf16[8192,4008]{0,1:T(8,128)(2,1)} %param.9), kind=kOutput, calls=%fused_computation.26 | convolution fusion | flops 3152412672 | bytes 12072960 | tf_op jit(solution)/shard_map/dot_general | solution.py:296
  197.4 1.9 select_bitcast_fusion.1
  199.3 1.9 select_bitcast_fusion.2
  220.3 3.0 %collective-permute-done.8 = bf16[2,48,1024]{2,1,0:T(8,128)(2,1)S(1)} collective-permute-done((bf16[2,48,1024]{2,1,0:T(8,128)(2,1)S(1)}, bf16[2,48,1024]{2,1,0:T(8,128)(2,1)S(1)}, u32[]{:S(2)}, u32[]{:S(2)}) %collective-permute-start.8) | collective-permute-done | bytes 196640 | tf_op jit(solution)/shard_map/ppermute | solution.py:186
  224.5 3.0 %collective-permute-done.4 = bf16[2,48,1024]{2,1,0:T(8,128)(2,1)S(1)} collective-permute-done((bf16[2,48,1024]{2,1,0:T(8,128)(2,1)S(1)}, bf16[2,48,1024]{2,1,0:T(8,128)(2,1)S(1)}, u32[]{:S(2)}, u32[]{:S(2)}) %collective-permute-start.4) | collective-permute-done | bytes 196640 | tf_op jit(solution)/shard_map/ppermute | solution.py:186
  228.7 2.2 collective-permute-done.1
  235.6 2.4 collective-permute-done.16
  250.3 2.4 collective-permute-done.6
  255.4 2.5 collective-permute-start.29
  259.3 2.6 collective-permute-done.29
  (180 shorter events, 59.3 us)
Async XLA Ops:
  143.3 63.1 %collective-permute-start.10 = (bf16[2,2,48,1024]{3,2,0,1:T(8,128)(2,1)}, bf16[2,2,48,1024]{3,2,0,1:T(8,128)(2,1)}, u32[]{:S(2)}, u32[]{:S(2)}) collective-permute-start(bf16[2,2,48,1024]{3,2,0,1:T(8,128)(2,1)} %select_bitcast_fusion.4), channel_id=1, source_target_pairs={{0,4},{4,0},{8,12},{12,8},{16,20},{20,16},{24,28},{28,24},{1,5},{5... | collective-permute-start | bytes 1179656 | tf_op jit(solution)/shard_map/ppermute | solution.py:186
  152.0 56.1 %collective-permute-start.7 = (bf16[2,2,48,1024]{3,2,0,1:T(8,128)(2,1)}, bf16[2,2,48,1024]{3,2,0,1:T(8,128)(2,1)}, u32[]{:S(2)}, u32[]{:S(2)}) collective-permute-start(bf16[2,2,48,1024]{3,2,0,1:T(8,128)(2,1)} %select_bitcast_fusion.5), channel_id=1, source_target_pairs={{0,4},{4,0},{8,12},{12,8},{16,20},{20,16},{24,28},{28,24},{1,5},{5... | collective-permute-start | bytes 1179656 | tf_op jit(solution)/shard_map/ppermute | solution.py:186
  159.3 50.3 %collective-permute-start.3 = (bf16[2,2,48,1024]{3,2,0,1:T(8,128)(2,1)}, bf16[2,2,48,1024]{3,2,0,1:T(8,128)(2,1)}, u32[]{:S(2)}, u32[]{:S(2)}) collective-permute-start(bf16[2,2,48,1024]{3,2,0,1:T(8,128)(2,1)} %select_bitcast_fusion.6), channel_id=1, source_target_pairs={{0,4},{4,0},{8,12},{12,8},{16,20},{20,16},{24,28},{28,24},{1,5},{5... | collective-permute-start | bytes 1179656 | tf_op jit(solution)/shard_map/ppermute | solution.py:186
  166.4 44.9 %collective-permute-start = (bf16[2,2,48,1024]{3,2,0,1:T(8,128)(2,1)}, bf16[2,2,48,1024]{3,2,0,1:T(8,128)(2,1)}, u32[]{:S(2)}, u32[]{:S(2)}) collective-permute-start(bf16[2,2,48,1024]{3,2,0,1:T(8,128)(2,1)} %select_bitcast_fusion.7), channel_id=1, source_target_pairs={{0,4},{4,0},{8,12},{12,8},{16,20},{20,16},{24,28},{28,24},{1,5},{5... | collective-permute-start | bytes 1179656 | tf_op jit(solution)/shard_map/ppermute | solution.py:186
  174.7 38.9 %collective-permute-start.25 = (bf16[2,2,48,1024]{3,2,1,0:T(8,128)(2,1)}, bf16[2,2,48,1024]{3,2,1,0:T(8,128)(2,1)S(1)}, u32[]{:S(2)}, u32[]{:S(2)}) collective-permute-start(bf16[2,2,48,1024]{3,2,1,0:T(8,128)(2,1)} %select_bitcast_fusion), channel_id=1, source_target_pairs={{0,4},{4,0},{8,12},{12,8},{16,20},{20,16},{24,28},{28,24},{1,5},{5... | collective-permute-start | bytes 1179656 | tf_op jit(solution)/shard_map/ppermute | solution.py:186
  206.5 8.5 %collective-permute-start.22 = (bf16[2,2,48,1024]{3,2,1,0:T(8,128)(2,1)}, bf16[2,2,48,1024]{3,2,1,0:T(8,128)(2,1)S(1)}, u32[]{:S(2)}, u32[]{:S(2)}) collective-permute-start(bf16[2,2,48,1024]{3,2,1,0:T(8,128)(2,1)} %select_bitcast_fusion.1), channel_id=1, source_target_pairs={{0,4},{4,0},{8,12},{12,8},{16,20},{20,16},{24,28},{28,24},{1,5},{5... | collective-permute-start | bytes 1179656 | tf_op jit(solution)/shard_map/ppermute | solution.py:186
  208.2 8.1 %collective-permute-start.18 = (bf16[2,2,48,1024]{3,2,1,0:T(8,128)(2,1)}, bf16[2,2,48,1024]{3,2,1,0:T(8,128)(2,1)S(1)}, u32[]{:S(2)}, u32[]{:S(2)}) collective-permute-start(bf16[2,2,48,1024]{3,2,1,0:T(8,128)(2,1)} %select_bitcast_fusion.2), channel_id=1, source_target_pairs={{0,4},{4,0},{8,12},{12,8},{16,20},{20,16},{24,28},{28,24},{1,5},{5... | collective-permute-start | bytes 1179656 | tf_op jit(solution)/shard_map/ppermute | solution.py:186
  209.6 8.0 %collective-permute-start.15 = (bf16[2,2,48,1024]{3,2,1,0:T(8,128)(2,1)S(1)}, bf16[2,2,48,1024]{3,2,1,0:T(8,128)(2,1)S(1)}, u32[]{:S(2)}, u32[]{:S(2)}) collective-permute-start(bf16[2,2,48,1024]{3,2,1,0:T(8,128)(2,1)S(1)} %select_bitcast_fusion.3), channel_id=1, source_target_pairs={{0,4},{4,0},{8,12},{12,8},{16,20},{20,16},{24,28},{28,24},{1,5},{5... | collective-permute-start | bytes 1179656 | tf_op jit(solution)/shard_map/ppermute | solution.py:186
  211.3 7.8 %collective-permute-start.11 = (bf16[2,48,1024]{2,1,0:T(8,128)(2,1)S(1)}, bf16[2,48,1024]{2,1,0:T(8,128)(2,1)S(1)}, u32[]{:S(2)}, u32[]{:S(2)}) collective-permute-start(bf16[2,48,1024]{2,1,0:T(8,128)(2,1)S(1)} %select_bitcast_fusion.12), channel_id=1, source_target_pairs={{0,8},{4,12},{8,0},{12,4},{16,24},{20,28},{24,16},{28,20},{1,9},{5... | collective-permute-start | bytes 589832 | tf_op jit(solution)/shard_map/ppermute | solution.py:186
  213.6 9.7 %collective-permute-start.8 = (bf16[2,48,1024]{2,1,0:T(8,128)(2,1)S(1)}, bf16[2,48,1024]{2,1,0:T(8,128)(2,1)S(1)}, u32[]{:S(2)}, u32[]{:S(2)}) collective-permute-start(bf16[2,48,1024]{2,1,0:T(8,128)(2,1)S(1)} %select_bitcast_fusion.13), channel_id=1, source_target_pairs={{0,8},{4,12},{8,0},{12,4},{16,24},{20,28},{24,16},{28,20},{1,9},{5... | collective-permute-start | bytes 589832 | tf_op jit(solution)/shard_map/ppermute | solution.py:186
  214.9 12.6 %collective-permute-start.4 = (bf16[2,48,1024]{2,1,0:T(8,128)(2,1)S(1)}, bf16[2,48,1024]{2,1,0:T(8,128)(2,1)S(1)}, u32[]{:S(2)}, u32[]{:S(2)}) collective-permute-start(bf16[2,48,1024]{2,1,0:T(8,128)(2,1)S(1)} %select_bitcast_fusion.14), channel_id=1, source_target_pairs={{0,8},{4,12},{8,0},{12,4},{16,24},{20,28},{24,16},{28,20},{1,9},{5... | collective-permute-start | bytes 589832 | tf_op jit(solution)/shard_map/ppermute | solution.py:186
  216.3 14.7 %collective-permute-start.1 = (bf16[2,48,1024]{2,1,0:T(8,128)(2,1)S(1)}, bf16[2,48,1024]{2,1,0:T(8,128)(2,1)S(1)}, u32[]{:S(2)}, u32[]{:S(2)}) collective-permute-start(bf16[2,48,1024]{2,1,0:T(8,128)(2,1)S(1)} %select_bitcast_fusion.15), channel_id=1, source_target_pairs={{0,8},{4,12},{8,0},{12,4},{16,24},{20,28},{24,16},{28,20},{1,9},{5... | collective-permute-start | bytes 589832 | tf_op jit(solution)/shard_map/ppermute | solution.py:186
  217.6 14.6 %collective-permute-start.26 = (bf16[2,48,1024]{2,1,0:T(8,128)(2,1)S(1)}, bf16[2,48,1024]{2,1,0:T(8,128)(2,1)S(1)}, u32[]{:S(2)}, u32[]{:S(2)}) collective-permute-start(bf16[2,48,1024]{2,1,0:T(8,128)(2,1)S(1)} %select_bitcast_fusion.8), channel_id=1, source_target_pairs={{0,16},{4,20},{8,24},{12,28},{16,0},{20,4},{24,8},{28,12},{1,17},{... | collective-permute-start | bytes 589832 | tf_op jit(solution)/shard_map/ppermute | solution.py:186
  219.1 14.1 %collective-permute-start.23 = (bf16[2,48,1024]{2,1,0:T(8,128)(2,1)S(1)}, bf16[2,48,1024]{2,1,0:T(8,128)(2,1)S(1)}, u32[]{:S(2)}, u32[]{:S(2)}) collective-permute-start(bf16[2,48,1024]{2,1,0:T(8,128)(2,1)S(1)} %select_bitcast_fusion.9), channel_id=1, source_target_pairs={{0,16},{4,20},{8,24},{12,28},{16,0},{20,4},{24,8},{28,12},{1,17},{... | collective-permute-start | bytes 589832 | tf_op jit(solution)/shard_map/ppermute | solution.py:186
  223.3 11.2 %collective-permute-start.19 = (bf16[2,48,1024]{2,1,0:T(8,128)(2,1)S(1)}, bf16[2,48,1024]{2,1,0:T(8,128)(2,1)S(1)}, u32[]{:S(2)}, u32[]{:S(2)}) collective-permute-start(bf16[2,48,1024]{2,1,0:T(8,128)(2,1)S(1)} %select_bitcast_fusion.10), channel_id=1, source_target_pairs={{0,16},{4,20},{8,24},{12,28},{16,0},{20,4},{24,8},{28,12},{1,17},{... | collective-permute-start | bytes 589832 | tf_op jit(solution)/shard_map/ppermute | solution.py:186
  227.5 10.5 %collective-permute-start.16 = (bf16[2,48,1024]{2,1,0:T(8,128)(2,1)S(1)}, bf16[2,48,1024]{2,1,0:T(8,128)(2,1)S(1)}, u32[]{:S(2)}, u32[]{:S(2)}) collective-permute-start(bf16[2,48,1024]{2,1,0:T(8,128)(2,1)S(1)} %select_bitcast_fusion.11), channel_id=1, source_target_pairs={{0,16},{4,20},{8,24},{12,28},{16,0},{20,4},{24,8},{28,12},{1,17},{... | collective-permute-start | bytes 589832 | tf_op jit(solution)/shard_map/ppermute | solution.py:186
  230.9 9.2 %collective-permute-start.12 = (bf16[48,1024]{1,0:T(8,128)(2,1)S(1)}, bf16[48,1024]{1,0:T(8,128)(2,1)S(1)}, u32[]{:S(2)}, u32[]{:S(2)}) collective-permute-start(bf16[48,1024]{1,0:T(8,128)(2,1)S(1)} %select_bitcast_fusion.20), channel_id=1, source_target_pairs={{0,16},{4,20},{8,24},{12,28},{16,0},{20,4},{24,8},{28,12},{1,17},{... | collective-permute-start | bytes 294920 | tf_op jit(solution)/shard_map/ppermute | solution.py:186
  232.2 10.1 %collective-permute-start.9 = (bf16[48,1024]{1,0:T(8,128)(2,1)S(1)}, bf16[48,1024]{1,0:T(8,128)(2,1)S(1)}, u32[]{:S(2)}, u32[]{:S(2)}) collective-permute-start(bf16[48,1024]{1,0:T(8,128)(2,1)S(1)} %select_bitcast_fusion.21), channel_id=1, source_target_pairs={{0,16},{4,20},{8,24},{12,28},{16,0},{20,4},{24,8},{28,12},{1,17},{... | collective-permute-start | bytes 294920 | tf_op jit(solution)/shard_map/ppermute | solution.py:186
  233.3 10.2 %collective-permute-start.5 = (bf16[48,1024]{1,0:T(8,128)(2,1)S(1)}, bf16[48,1024]{1,0:T(8,128)(2,1)S(1)}, u32[]{:S(2)}, u32[]{:S(2)}) collective-permute-start(bf16[48,1024]{1,0:T(8,128)(2,1)S(1)} %select_bitcast_fusion.22), channel_id=1, source_target_pairs={{0,16},{4,20},{8,24},{12,28},{16,0},{20,4},{24,8},{28,12},{1,17},{... | collective-permute-start | bytes 294920 | tf_op jit(solution)/shard_map/ppermute | solution.py:186
  234.6 10.1 %collective-permute-start.2 = (bf16[48,1024]{1,0:T(8,128)(2,1)S(1)}, bf16[48,1024]{1,0:T(8,128)(2,1)S(1)}, u32[]{:S(2)}, u32[]{:S(2)}) collective-permute-start(bf16[48,1024]{1,0:T(8,128)(2,1)S(1)} %select_bitcast_fusion.23), channel_id=1, source_target_pairs={{0,16},{4,20},{8,24},{12,28},{16,0},{20,4},{24,8},{28,12},{1,17},{... | collective-permute-start | bytes 294920 | tf_op jit(solution)/shard_map/ppermute | solution.py:186
  238.1 7.5 %collective-permute-start.27 = (bf16[48,1024]{1,0:T(8,128)(2,1)S(1)}, bf16[48,1024]{1,0:T(8,128)(2,1)S(1)}, u32[]{:S(2)}, u32[]{:S(2)}) collective-permute-start(bf16[48,1024]{1,0:T(8,128)(2,1)S(1)} %select_bitcast_fusion.16), channel_id=1, source_target_pairs={{0,8},{4,12},{8,0},{12,4},{16,24},{20,28},{24,16},{28,20},{1,9},{5... | collective-permute-start | bytes 294920 | tf_op jit(solution)/shard_map/ppermute | solution.py:186
  245.6 7.1 %collective-permute-start.6 = (bf16[48,1024]{1,0:T(8,128)(2,1)S(1)}, bf16[48,1024]{1,0:T(8,128)(2,1)S(1)}, u32[]{:S(2)}, u32[]{:S(2)}) collective-permute-start(bf16[48,1024]{1,0:T(8,128)(2,1)S(1)} %get-tuple-element.16), channel_id=1, source_target_pairs={{0,1},{1,0},{2,3},{3,2},{4,5},{5,4},{6,7},{7,6},{8,9},{9,8},{10,11... | collective-permute-start | bytes 294920 | tf_op jit(solution)/shard_map/ppermute | solution.py:186
  246.9 7.3 %collective-permute-start.28 = (bf16[48,1024]{1,0:T(8,128)(2,1)S(1)}, bf16[48,1024]{1,0:T(8,128)(2,1)S(1)}, u32[]{:S(2)}, u32[]{:S(2)}) collective-permute-start(bf16[48,1024]{1,0:T(8,128)(2,1)S(1)} %get-tuple-element.28), channel_id=1, source_target_pairs={{0,1},{1,0},{2,3},{3,2},{4,5},{5,4},{6,7},{7,6},{8,9},{9,8},{10,11... | collective-permute-start | bytes 294920 | tf_op jit(solution)/shard_map/ppermute | solution.py:186
  248.2 7.1 %collective-permute-start.21 = (bf16[48,1024]{1,0:T(8,128)(2,1)S(1)}, bf16[48,1024]{1,0:T(8,128)(2,1)S(1)}, u32[]{:S(2)}, u32[]{:S(2)}) collective-permute-start(bf16[48,1024]{1,0:T(8,128)(2,1)S(1)} %get-tuple-element.25), channel_id=1, source_target_pairs={{0,1},{1,0},{2,3},{3,2},{4,5},{5,4},{6,7},{7,6},{8,9},{9,8},{10,11... | collective-permute-start | bytes 294920 | tf_op jit(solution)/shard_map/ppermute | solution.py:186
  (17 other events, 210.6 us)
where the time goes:
time: 264 us; the launch traced here: 263 us
  matrix products  110 us (42%)
  Pallas kernels  60.8 us (23%)
  other arithmetic  34.9 us (13%)
  starting transfers between devices  27.2 us (10%)
  waiting for transfers between devices  21.8 us (8%)
  local copies, waits for them, and re-layouts  6.44 us (2%)
    dot_general x8, matrix products, on_device(): lax.dot_general(grad_logits, weight, (((1,), (1,)), ((), ())), preferred_...  55.9 us
    pallas_call x1, Pallas kernels, gather(): pl.pallas_call(functools.partial(gather_kernel, ranks_dp, ranks_vocab), o...  45.7 us
    dot_general x1, matrix products, on_device(): jnp.dot(hidden_all, head_weight, preferred_element_type=jnp.float32)  42.2 us
    ppermute x30, starting transfers between devices, halve(): lax.ppermute(sent, axis_name, [(i, i ^ 1 << bit) for i in range(ranks)])  27.2 us
    ppermute x30, waiting for transfers between devices, halve(): lax.ppermute(sent, axis_name, [(i, i ^ 1 << bit) for i in range(ranks)])  21.8 us
    pallas_call x1, Pallas kernels, exchange(): pl.pallas_call(functools.partial(exchange_kernel, ranks_dp, ranks_vocab,...  15.1 us
    select_n x30, other arithmetic, halve(): sent = jnp.where(mine == 0, second, first)  9.84 us
    dot_general x1, matrix products, on_device(): inner = jnp.dot(normed, critic_in[0], preferred_element_type=jnp.float32)  8.28 us
  transfers between devices with their start and end apart: 30, of which 14 were waited for; matrix products, arithmetic and copies ran while one was open for 26% of the time, Pallas kernels for 0%

commit v1 on v0

--- a/solution.py
+++ b/solution.py
@@ -17,55 +17,55 @@
     return values * lax.rsqrt(jnp.mean(values * values, axis=-1, keepdims=True) + epsilon)
 
 
-def exchange_kernel(ranks_dp, ranks_vocab, over_vocab, block_ref, all_ref, send_sem, recv_sem, own_sem):
-    my_dp, my_vocab = lax.axis_index("dp"), lax.axis_index("vocab")
-    count = ranks_dp * ranks_vocab if over_vocab else ranks_dp
-    me = my_dp * ranks_vocab + my_vocab if over_vocab else my_dp
-
-    def place(step):
-        peer = lax.rem(me + step, count)
-        if over_vocab:
-            return (lax.div(peer, ranks_vocab), lax.rem(peer, ranks_vocab))
-        return (peer, my_vocab)
-
+def exchange_kernel(ranks_dp, ranks_vocab, block_ref, all_ref, send_sem, recv_sem, own_sem):
+    me, col = lax.axis_index("dp"), lax.axis_index("vocab")
+    across = [(me, col ^ step) for step in range(1, ranks_vocab)]
+    along = [(me ^ step, col) for step in range(1, ranks_dp)]
     barrier = pltpu.get_barrier_semaphore()
-    for step in range(1, count):
-        pl.semaphore_signal(barrier, inc=1, device_id=place(step), device_id_type=MESH)
-    pl.semaphore_wait(barrier, count - 1)
-    own = pltpu.make_async_copy(block_ref, all_ref.at[me], own_sem)
+    for peer in across + along:
+        pl.semaphore_signal(barrier, inc=1, device_id=peer, device_id_type=MESH)
+    pl.semaphore_wait(barrier, ranks_dp + ranks_vocab - 2)
+    own = pltpu.make_async_copy(block_ref, all_ref.at[me, col], own_sem)
     own.start()
-    copies = []
-    for step in range(1, count):
-        copy = pltpu.make_async_remote_copy(
-            src_ref=block_ref,
-            dst_ref=all_ref.at[me],
-            send_sem=send_sem.at[step],
-            recv_sem=recv_sem.at[step],
-            device_id=place(step),
-            device_id_type=MESH,
-        )
-        copy.start()
-        copies.append(copy)
+
+    def send(source, target, peers, first):
+        copies = []
+        for number, peer in enumerate(peers):
+            copy = pltpu.make_async_remote_copy(
+                src_ref=source,
+                dst_ref=target,
+                send_sem=send_sem.at[first + number],
+                recv_sem=recv_sem.at[first + number],
+                device_id=peer,
+                device_id_type=MESH,
+            )
+            copy.start()
+            copies.append(copy)
+        return copies
+
+    for copy in send(block_ref, all_ref.at[me, col], across, 0):
+        copy.wait()
     own.wait()
-    for copy in copies:
+    for copy in send(all_ref.at[me], all_ref.at[me], along, len(across)):
         copy.wait()
 
 
-def exchange(block, over_vocab, collective_id):
+def exchange(block, collective_id):
     ranks_dp, ranks_vocab = lax.axis_size("dp"), lax.axis_size("vocab")
-    count = ranks_dp * ranks_vocab if over_vocab else ranks_dp
-    return pl.pallas_call(
-        functools.partial(exchange_kernel, ranks_dp, ranks_vocab, over_vocab),
-        out_shape=jax.ShapeDtypeStruct((count,) + block.shape, block.dtype),
+    copies = ranks_dp + ranks_vocab - 2
+    everything = pl.pallas_call(
+        functools.partial(exchange_kernel, ranks_dp, ranks_vocab),
+        out_shape=jax.ShapeDtypeStruct((ranks_dp, ranks_vocab) + block.shape, block.dtype),
         in_specs=[pl.BlockSpec(memory_space=pltpu.VMEM)],
         out_specs=pl.BlockSpec(memory_space=pltpu.VMEM),
         scratch_shapes=[
-            pltpu.SemaphoreType.DMA((count,)),
-            pltpu.SemaphoreType.DMA((count,)),
+            pltpu.SemaphoreType.DMA((copies,)),
+            pltpu.SemaphoreType.DMA((copies,)),
             pltpu.SemaphoreType.DMA,
         ],
         compiler_params=pltpu.CompilerParams(collective_id=collective_id, has_side_effects=True),
     )(block)
+    return everything.reshape((-1,) + block.shape)
 
 
 def gather_kernel(
@@ -264,7 +264,7 @@
         [top_part, mass_part, picked_part, jnp.pad(value_part, (0, tokens - per_critic))]
         + [jnp.zeros((tokens,), jnp.float32)] * 4
     )
-    stats = exchange(stats, True, 2)
+    stats = exchange(stats, 2)
     row_top = jnp.max(stats[:, 0], axis=0)
     row_mass = jnp.sum(stats[:, 1] * jnp.exp(stats[:, 0] - row_top[None, :]), axis=0)
     picked = jnp.sum(stats[:, 2], axis=0)

time: 264 us -> 261 us (0.989)
  waiting for transfers between devices: 21.8 us -> 27.9 us
  starting transfers between devices: 27.2 us -> 21.3 us
    ppermute x30, waiting for transfers between devices: 21.8 us -> 27.9 us  [halve(): lax.ppermute(sent, axis_name, [(i, i ^ 1 << bit) for i in range(ranks)])]
    ppermute x30, starting transfers between devices: 27.2 us -> 21.3 us  [halve(): lax.ppermute(sent, axis_name, [(i, i ^ 1 << bit) for i in range(ranks)])]
  transfers between devices with their start and end apart: 30 -> 30, of which waited for: 14 -> 16; matrix products, arithmetic and copies ran while one was open for 26% -> 26% of each run, Pallas kernels for 0% -> 0%
where the time goes in v1:
time: 261 us; the launch traced here: 260 us
  matrix products  110 us (42%)
  Pallas kernels  58.3 us (22%)
  other arithmetic  34.9 us (13%)
  waiting for transfers between devices  27.9 us (11%)
  starting transfers between devices  21.3 us (8%)
  local copies, waits for them, and re-layouts  6.44 us (2%)
    dot_general x8, matrix products, on_device(): lax.dot_general(grad_logits, weight, (((1,), (1,)), ((), ())), preferred_...  55.9 us
    pallas_call x1, Pallas kernels, gather(): pl.pallas_call(functools.partial(gather_kernel, ranks_dp, ranks_vocab), o...  45.7 us
    dot_general x1, matrix products, on_device(): jnp.dot(hidden_all, head_weight, preferred_element_type=jnp.float32)  42.2 us
    ppermute x30, waiting for transfers between devices, halve(): lax.ppermute(sent, axis_name, [(i, i ^ 1 << bit) for i in range(ranks)])  27.9 us
    ppermute x30, starting transfers between devices, halve(): lax.ppermute(sent, axis_name, [(i, i ^ 1 << bit) for i in range(ranks)])  21.3 us
    pallas_call x1, Pallas kernels, exchange(): pl.pallas_call(functools.partial(exchange_kernel, ranks_dp, ranks_vocab),...  12.6 us
    select_n x30, other arithmetic, halve(): sent = jnp.where(mine == 0, second, first)  9.84 us
    dot_general x1, matrix products, on_device(): inner = jnp.dot(normed, critic_in[0], preferred_element_type=jnp.float32)  8.28 us
  transfers between devices with their start and end apart: 30, of which 16 were waited for; matrix products, arithmetic and copies ran while one was open for 26% of the time, Pallas kernels for 0%

profile of v1, /device:TPU:0, one launch (start us, length us, event | category | flops | bytes accessed | tf_op | source)
XLA Modules:
  0.0 260.4 jit_solution(17781231051020875689)
XLA Ops:
  3.4 45.7 %shard_map.103 = (bf16[8,48,8192]{2,1,0:T(8,128)(2,1)}, f32[8,8,128]{2,1,0:T(8,128)}) custom-call(bf16[48,2048]{1,0:T(8,128)(2,1)} %x_ref.1, f32[8,128]{1,0:T(8,128)} %maximum_maximum_fusion.facts_ref), custom_call_target="tpu_custom_call" | custom-call | tf_op jit(solution)/shard_map/pallas_call | solution.py:158
  53.0 3.9 %multiply_reduce_fusion = (f32[24]{0:T(128)S(1)}, f32[24,8192]{1,0:T(8,128)S(1)}) fusion(bf16[384,8192]{1,0:T(8,128)(2,1)} %bitcast.234, s32[24]{0:T(128)S(1)} %broadcast_add_fusion), kind=kOutput, calls=%fused_computation.47 | convolution fusion | flops 151397344 | bytes 7078080 | tf_op jit(solution)/shard_map/dot_general | solution.py:248
  56.9 8.3 %multiply_reduce_fusion.1 = f32[24]{0:T(128)S(1)} fusion(bf16[1,8192,1024]{2,1,0:T(8,128)(2,1)} %param.10, f32[24,8192]{1,0:T(8,128)S(1)} %get-tuple-element.46, f32[24]{0:T(128)S(1)} %add_rsqrt_fusion, f32[1024]{0:T(1024)S(1)} %bitcast.256), kind=kOutput, calls=%fused_computation.122 | convolution fusion | flops 403242976 | bytes 17567936 | tf_op jit(solution)/shard_map/dot_general | solution.py:250
  65.2 42.2 %fusion.90 = (f32[384]{0:T(512)S(1)}, f32[384,4008]{0,1:T(8,128)}) fusion(bf16[384,8192]{1,0:T(8,128)(2,1)} %bitcast.235, bf16[8192,4008]{0,1:T(8,128)(2,1)} %param.9), kind=kOutput, calls=%fused_computation.174 | convolution fusion | flops 25217693696 | bytes 78116352 | tf_op jit(solution)/shard_map/dot_general | solution.py:256
  107.4 4.4 %select_reduce_fusion = (f32[384]{0:T(512)S(1)}, f32[384]{0:T(512)S(1)}) fusion(f32[384,4008]{0,1:T(8,128)} %get-tuple-element.44, s32[384]{0:T(512)S(1)} %broadcast_subtract_fusion, f32[384]{0:T(512)S(1)} %get-tuple-element.43), kind=kLoop, calls=%fused_computation.19 | loop fusion | flops 7694592 | bytes 6162432 | tf_op jit(solution)/shard_map/reduce_sum | solution.py:259
  112.5 12.6 %shard_map.104 = f32[8,4,8,384]{3,2,1,0:T(8,128)} custom-call(f32[8,384]{1,0:T(8,128)} %stack.23.block_ref), custom_call_target="tpu_custom_call" | custom-call | tf_op jit(solution)/shard_map/pallas_call | solution.py:56
  128.1 4.7 %multiply_convert_fusion = bf16[384,4008]{0,1:T(8,128)(2,1)S(1)} fusion(f32[384,4008]{0,1:T(8,128)} %get-tuple-element.44, f32[384]{0:T(512)S(1)} %fusion.74, f32[384]{0:T(512)S(1)} %get-tuple-element.10, f32[384]{0:T(512)S(1)} %subtract_multiply_fusion, s32[384]{0:T(512)S(1)} %broadcast_subtract_fusion), kind=kLoop, calls=%fused_computation.18 | loop fusion | flops 10773504 | bytes 9240576 | tf_op jit(solution)/shard_map/convert_element_type | solution.py:285
  132.8 7.2 %fusion.27 = bf16[384,1024]{1,0:T(8,128)(2,1)S(1)} fusion(bf16[384,4008]{0,1:T(8,128)(2,1)S(1)} %multiply_convert_fusion, bf16[8192,4008]{0,1:T(8,128)(2,1)} %param.9), kind=kOutput, calls=%fused_computation.25 | convolution fusion | flops 3152412672 | bytes 12072960 | tf_op jit(solution)/shard_map/dot_general | solution.py:296
  141.1 7.9 %fusion.24 = bf16[384,1024]{1,0:T(8,128)(2,1)S(1)} fusion(bf16[384,4008]{0,1:T(8,128)(2,1)} %copy-done.5, bf16[8192,4008]{0,1:T(8,128)(2,1)} %param.9), kind=kOutput, calls=%fused_computation.24 | convolution fusion | flops 3152412672 | bytes 12072960 | tf_op jit(solution)/shard_map/dot_general | solution.py:296
  150.0 6.0 %fusion.21 = bf16[384,1024]{1,0:T(8,128)(2,1)S(1)} fusion(bf16[384,4008]{0,1:T(8,128)(2,1)S(1)} %copy-done.6, bf16[8192,4008]{0,1:T(8,128)(2,1)} %param.9), kind=kOutput, calls=%fused_computation.23 | convolution fusion | flops 3152412672 | bytes 12072960 | tf_op jit(solution)/shard_map/dot_general | solution.py:296
  157.3 6.0 %fusion.18 = bf16[384,1024]{1,0:T(8,128)(2,1)S(1)} fusion(bf16[384,4008]{0,1:T(8,128)(2,1)S(1)} %copy-done.6, bf16[8192,4008]{0,1:T(8,128)(2,1)} %param.9), kind=kOutput, calls=%fused_computation.22 | convolution fusion | flops 3152412672 | bytes 12072960 | tf_op jit(solution)/shard_map/dot_general | solution.py:296
  164.4 6.3 %fusion.39 = bf16[384,1024]{1,0:T(8,128)(2,1)S(1)} fusion(bf16[384,4008]{0,1:T(8,128)(2,1)S(1)} %copy-done.6, bf16[8192,4008]{0,1:T(8,128)(2,1)} %param.9), kind=kOutput, calls=%fused_computation.29 | convolution fusion | flops 3152412672 | bytes 12072960 | tf_op jit(solution)/shard_map/dot_general | solution.py:296
  172.7 8.7 %fusion.36 = bf16[384,1024]{1,0:T(8,128)(2,1)} fusion(bf16[384,4008]{0,1:T(8,128)(2,1)} %copy-done.5, bf16[8192,4008]{0,1:T(8,128)(2,1)} %param.9), kind=kOutput, calls=%fused_computation.28 | convolution fusion | flops 3152412672 | bytes 12072960 | tf_op jit(solution)/shard_map/dot_general | solution.py:296
  181.4 6.9 %fusion.33 = bf16[384,1024]{1,0:T(8,128)(2,1)} fusion(bf16[384,4008]{0,1:T(8,128)(2,1)S(1)} %copy-done.7, bf16[8192,4008]{0,1:T(8,128)(2,1)} %param.9), kind=kOutput, calls=%fused_computation.27 | convolution fusion | flops 3152412672 | bytes 12072960 | tf_op jit(solution)/shard_map/dot_general | solution.py:296
  188.4 6.9 %fusion.30 = bf16[384,1024]{1,0:T(8,128)(2,1)} fusion(bf16[384,4008]{0,1:T(8,128)(2,1)S(1)} %copy-done.7, bf16[8192,4008]{0,1:T(8,128)(2,1)} %param.9), kind=kOutput, calls=%fused_computation.26 | convolution fusion | flops 3152412672 | bytes 12072960 | tf_op jit(solution)/shard_map/dot_general | solution.py:296
  195.3 1.9 select_bitcast_fusion.1
  197.2 1.9 select_bitcast_fusion.2
  217.7 3.2 %collective-permute-done.8 = bf16[2,48,1024]{2,1,0:T(8,128)(2,1)S(1)} collective-permute-done((bf16[2,48,1024]{2,1,0:T(8,128)(2,1)S(1)}, bf16[2,48,1024]{2,1,0:T(8,128)(2,1)S(1)}, u32[]{:S(2)}, u32[]{:S(2)}) %collective-permute-start.8) | collective-permute-done | bytes 196640 | tf_op jit(solution)/shard_map/ppermute | solution.py:186
  221.7 3.5 %collective-permute-done.4 = bf16[2,48,1024]{2,1,0:T(8,128)(2,1)S(1)} collective-permute-done((bf16[2,48,1024]{2,1,0:T(8,128)(2,1)S(1)}, bf16[2,48,1024]{2,1,0:T(8,128)(2,1)S(1)}, u32[]{:S(2)}, u32[]{:S(2)}) %collective-permute-start.4) | collective-permute-done | bytes 196640 | tf_op jit(solution)/shard_map/ppermute | solution.py:186
  225.9 2.9 %collective-permute-done.1 = bf16[2,48,1024]{2,1,0:T(8,128)(2,1)S(1)} collective-permute-done((bf16[2,48,1024]{2,1,0:T(8,128)(2,1)S(1)}, bf16[2,48,1024]{2,1,0:T(8,128)(2,1)S(1)}, u32[]{:S(2)}, u32[]{:S(2)}) %collective-permute-start.1) | collective-permute-done | bytes 196640 | tf_op jit(solution)/shard_map/ppermute | solution.py:186
  233.5 2.2 collective-permute-done.16
  248.1 2.7 %collective-permute-done.6 = bf16[48,1024]{1,0:T(8,128)(2,1)S(1)} collective-permute-done((bf16[48,1024]{1,0:T(8,128)(2,1)S(1)}, bf16[48,1024]{1,0:T(8,128)(2,1)S(1)}, u32[]{:S(2)}, u32[]{:S(2)}) %collective-permute-start.6) | collective-permute-done | bytes 98336 | tf_op jit(solution)/shard_map/ppermute | solution.py:186
  254.3 2.8 %collective-permute-done.14 = bf16[48,1024]{1,0:T(8,128)(2,1)S(1)} collective-permute-done((bf16[48,1024]{1,0:T(8,128)(2,1)S(1)}, bf16[48,1024]{1,0:T(8,128)(2,1)S(1)}, u32[]{:S(2)}, u32[]{:S(2)}) %collective-permute-start.14) | collective-permute-done | bytes 98336 | tf_op jit(solution)/shard_map/ppermute | solution.py:186
  257.2 2.4 collective-permute-done.29
  (180 shorter events, 57.8 us)
Async XLA Ops:
  140.8 63.5 %collective-permute-start.10 = (bf16[2,2,48,1024]{3,2,0,1:T(8,128)(2,1)}, bf16[2,2,48,1024]{3,2,0,1:T(8,128)(2,1)}, u32[]{:S(2)}, u32[]{:S(2)}) collective-permute-start(bf16[2,2,48,1024]{3,2,0,1:T(8,128)(2,1)} %select_bitcast_fusion.4), channel_id=1, source_target_pairs={{0,4},{4,0},{8,12},{12,8},{16,20},{20,16},{24,28},{28,24},{1,5},{5... | collective-permute-start | bytes 1179656 | tf_op jit(solution)/shard_map/ppermute | solution.py:186
  149.9 55.9 %collective-permute-start.7 = (bf16[2,2,48,1024]{3,2,0,1:T(8,128)(2,1)}, bf16[2,2,48,1024]{3,2,0,1:T(8,128)(2,1)}, u32[]{:S(2)}, u32[]{:S(2)}) collective-permute-start(bf16[2,2,48,1024]{3,2,0,1:T(8,128)(2,1)} %select_bitcast_fusion.5), channel_id=1, source_target_pairs={{0,4},{4,0},{8,12},{12,8},{16,20},{20,16},{24,28},{28,24},{1,5},{5... | collective-permute-start | bytes 1179656 | tf_op jit(solution)/shard_map/ppermute | solution.py:186
  156.9 50.5 %collective-permute-start.3 = (bf16[2,2,48,1024]{3,2,0,1:T(8,128)(2,1)}, bf16[2,2,48,1024]{3,2,0,1:T(8,128)(2,1)}, u32[]{:S(2)}, u32[]{:S(2)}) collective-permute-start(bf16[2,2,48,1024]{3,2,0,1:T(8,128)(2,1)} %select_bitcast_fusion.6), channel_id=1, source_target_pairs={{0,4},{4,0},{8,12},{12,8},{16,20},{20,16},{24,28},{28,24},{1,5},{5... | collective-permute-start | bytes 1179656 | tf_op jit(solution)/shard_map/ppermute | solution.py:186
  164.2 44.7 %collective-permute-start = (bf16[2,2,48,1024]{3,2,0,1:T(8,128)(2,1)}, bf16[2,2,48,1024]{3,2,0,1:T(8,128)(2,1)}, u32[]{:S(2)}, u32[]{:S(2)}) collective-permute-start(bf16[2,2,48,1024]{3,2,0,1:T(8,128)(2,1)} %select_bitcast_fusion.7), channel_id=1, source_target_pairs={{0,4},{4,0},{8,12},{12,8},{16,20},{20,16},{24,28},{28,24},{1,5},{5... | collective-permute-start | bytes 1179656 | tf_op jit(solution)/shard_map/ppermute | solution.py:186
  172.3 38.4 %collective-permute-start.25 = (bf16[2,2,48,1024]{3,2,1,0:T(8,128)(2,1)}, bf16[2,2,48,1024]{3,2,1,0:T(8,128)(2,1)S(1)}, u32[]{:S(2)}, u32[]{:S(2)}) collective-permute-start(bf16[2,2,48,1024]{3,2,1,0:T(8,128)(2,1)} %select_bitcast_fusion), channel_id=1, source_target_pairs={{0,4},{4,0},{8,12},{12,8},{16,20},{20,16},{24,28},{28,24},{1,5},{5... | collective-permute-start | bytes 1179656 | tf_op jit(solution)/shard_map/ppermute | solution.py:186
  204.3 8.2 %collective-permute-start.22 = (bf16[2,2,48,1024]{3,2,1,0:T(8,128)(2,1)}, bf16[2,2,48,1024]{3,2,1,0:T(8,128)(2,1)S(1)}, u32[]{:S(2)}, u32[]{:S(2)}) collective-permute-start(bf16[2,2,48,1024]{3,2,1,0:T(8,128)(2,1)} %select_bitcast_fusion.1), channel_id=1, source_target_pairs={{0,4},{4,0},{8,12},{12,8},{16,20},{20,16},{24,28},{28,24},{1,5},{5... | collective-permute-start | bytes 1179656 | tf_op jit(solution)/shard_map/ppermute | solution.py:186
  205.8 7.6 %collective-permute-start.18 = (bf16[2,2,48,1024]{3,2,1,0:T(8,128)(2,1)}, bf16[2,2,48,1024]{3,2,1,0:T(8,128)(2,1)S(1)}, u32[]{:S(2)}, u32[]{:S(2)}) collective-permute-start(bf16[2,2,48,1024]{3,2,1,0:T(8,128)(2,1)} %select_bitcast_fusion.2), channel_id=1, source_target_pairs={{0,4},{4,0},{8,12},{12,8},{16,20},{20,16},{24,28},{28,24},{1,5},{5... | collective-permute-start | bytes 1179656 | tf_op jit(solution)/shard_map/ppermute | solution.py:186
  207.4 7.8 %collective-permute-start.15 = (bf16[2,2,48,1024]{3,2,1,0:T(8,128)(2,1)S(1)}, bf16[2,2,48,1024]{3,2,1,0:T(8,128)(2,1)S(1)}, u32[]{:S(2)}, u32[]{:S(2)}) collective-permute-start(bf16[2,2,48,1024]{3,2,1,0:T(8,128)(2,1)S(1)} %select_bitcast_fusion.3), channel_id=1, source_target_pairs={{0,4},{4,0},{8,12},{12,8},{16,20},{20,16},{24,28},{28,24},{1,5},{5... | collective-permute-start | bytes 1179656 | tf_op jit(solution)/shard_map/ppermute | solution.py:186
  208.9 7.8 %collective-permute-start.11 = (bf16[2,48,1024]{2,1,0:T(8,128)(2,1)S(1)}, bf16[2,48,1024]{2,1,0:T(8,128)(2,1)S(1)}, u32[]{:S(2)}, u32[]{:S(2)}) collective-permute-start(bf16[2,48,1024]{2,1,0:T(8,128)(2,1)S(1)} %select_bitcast_fusion.12), channel_id=1, source_target_pairs={{0,8},{4,12},{8,0},{12,4},{16,24},{20,28},{24,16},{28,20},{1,9},{5... | collective-permute-start | bytes 589832 | tf_op jit(solution)/shard_map/ppermute | solution.py:186
  210.8 10.2 %collective-permute-start.8 = (bf16[2,48,1024]{2,1,0:T(8,128)(2,1)S(1)}, bf16[2,48,1024]{2,1,0:T(8,128)(2,1)S(1)}, u32[]{:S(2)}, u32[]{:S(2)}) collective-permute-start(bf16[2,48,1024]{2,1,0:T(8,128)(2,1)S(1)} %select_bitcast_fusion.13), channel_id=1, source_target_pairs={{0,8},{4,12},{8,0},{12,4},{16,24},{20,28},{24,16},{28,20},{1,9},{5... | collective-permute-start | bytes 589832 | tf_op jit(solution)/shard_map/ppermute | solution.py:186
  212.6 12.6 %collective-permute-start.4 = (bf16[2,48,1024]{2,1,0:T(8,128)(2,1)S(1)}, bf16[2,48,1024]{2,1,0:T(8,128)(2,1)S(1)}, u32[]{:S(2)}, u32[]{:S(2)}) collective-permute-start(bf16[2,48,1024]{2,1,0:T(8,128)(2,1)S(1)} %select_bitcast_fusion.14), channel_id=1, source_target_pairs={{0,8},{4,12},{8,0},{12,4},{16,24},{20,28},{24,16},{28,20},{1,9},{5... | collective-permute-start | bytes 589832 | tf_op jit(solution)/shard_map/ppermute | solution.py:186
  213.4 15.3 %collective-permute-start.1 = (bf16[2,48,1024]{2,1,0:T(8,128)(2,1)S(1)}, bf16[2,48,1024]{2,1,0:T(8,128)(2,1)S(1)}, u32[]{:S(2)}, u32[]{:S(2)}) collective-permute-start(bf16[2,48,1024]{2,1,0:T(8,128)(2,1)S(1)} %select_bitcast_fusion.15), channel_id=1, source_target_pairs={{0,8},{4,12},{8,0},{12,4},{16,24},{20,28},{24,16},{28,20},{1,9},{5... | collective-permute-start | bytes 589832 | tf_op jit(solution)/shard_map/ppermute | solution.py:186
  215.2 14.3 %collective-permute-start.26 = (bf16[2,48,1024]{2,1,0:T(8,128)(2,1)S(1)}, bf16[2,48,1024]{2,1,0:T(8,128)(2,1)S(1)}, u32[]{:S(2)}, u32[]{:S(2)}) collective-permute-start(bf16[2,48,1024]{2,1,0:T(8,128)(2,1)S(1)} %select_bitcast_fusion.8), channel_id=1, source_target_pairs={{0,16},{4,20},{8,24},{12,28},{16,0},{20,4},{24,8},{28,12},{1,17},{... | collective-permute-start | bytes 589832 | tf_op jit(solution)/shard_map/ppermute | solution.py:186
  216.8 14.3 %collective-permute-start.23 = (bf16[2,48,1024]{2,1,0:T(8,128)(2,1)S(1)}, bf16[2,48,1024]{2,1,0:T(8,128)(2,1)S(1)}, u32[]{:S(2)}, u32[]{:S(2)}) collective-permute-start(bf16[2,48,1024]{2,1,0:T(8,128)(2,1)S(1)} %select_bitcast_fusion.9), channel_id=1, source_target_pairs={{0,16},{4,20},{8,24},{12,28},{16,0},{20,4},{24,8},{28,12},{1,17},{... | collective-permute-start | bytes 589832 | tf_op jit(solution)/shard_map/ppermute | solution.py:186
  221.0 10.9 %collective-permute-start.19 = (bf16[2,48,1024]{2,1,0:T(8,128)(2,1)S(1)}, bf16[2,48,1024]{2,1,0:T(8,128)(2,1)S(1)}, u32[]{:S(2)}, u32[]{:S(2)}) collective-permute-start(bf16[2,48,1024]{2,1,0:T(8,128)(2,1)S(1)} %select_bitcast_fusion.10), channel_id=1, source_target_pairs={{0,16},{4,20},{8,24},{12,28},{16,0},{20,4},{24,8},{28,12},{1,17},{... | collective-permute-start | bytes 589832 | tf_op jit(solution)/shard_map/ppermute | solution.py:186
  225.2 10.5 %collective-permute-start.16 = (bf16[2,48,1024]{2,1,0:T(8,128)(2,1)S(1)}, bf16[2,48,1024]{2,1,0:T(8,128)(2,1)S(1)}, u32[]{:S(2)}, u32[]{:S(2)}) collective-permute-start(bf16[2,48,1024]{2,1,0:T(8,128)(2,1)S(1)} %select_bitcast_fusion.11), channel_id=1, source_target_pairs={{0,16},{4,20},{8,24},{12,28},{16,0},{20,4},{24,8},{28,12},{1,17},{... | collective-permute-start | bytes 589832 | tf_op jit(solution)/shard_map/ppermute | solution.py:186
  228.8 9.0 %collective-permute-start.12 = (bf16[48,1024]{1,0:T(8,128)(2,1)S(1)}, bf16[48,1024]{1,0:T(8,128)(2,1)S(1)}, u32[]{:S(2)}, u32[]{:S(2)}) collective-permute-start(bf16[48,1024]{1,0:T(8,128)(2,1)S(1)} %select_bitcast_fusion.20), channel_id=1, source_target_pairs={{0,16},{4,20},{8,24},{12,28},{16,0},{20,4},{24,8},{28,12},{1,17},{... | collective-permute-start | bytes 294920 | tf_op jit(solution)/shard_map/ppermute | solution.py:186
  229.5 10.4 %collective-permute-start.9 = (bf16[48,1024]{1,0:T(8,128)(2,1)S(1)}, bf16[48,1024]{1,0:T(8,128)(2,1)S(1)}, u32[]{:S(2)}, u32[]{:S(2)}) collective-permute-start(bf16[48,1024]{1,0:T(8,128)(2,1)S(1)} %select_bitcast_fusion.21), channel_id=1, source_target_pairs={{0,16},{4,20},{8,24},{12,28},{16,0},{20,4},{24,8},{28,12},{1,17},{... | collective-permute-start | bytes 294920 | tf_op jit(solution)/shard_map/ppermute | solution.py:186
  231.1 10.2 %collective-permute-start.5 = (bf16[48,1024]{1,0:T(8,128)(2,1)S(1)}, bf16[48,1024]{1,0:T(8,128)(2,1)S(1)}, u32[]{:S(2)}, u32[]{:S(2)}) collective-permute-start(bf16[48,1024]{1,0:T(8,128)(2,1)S(1)} %select_bitcast_fusion.22), channel_id=1, source_target_pairs={{0,16},{4,20},{8,24},{12,28},{16,0},{20,4},{24,8},{28,12},{1,17},{... | collective-permute-start | bytes 294920 | tf_op jit(solution)/shard_map/ppermute | solution.py:186
  231.9 10.5 %collective-permute-start.2 = (bf16[48,1024]{1,0:T(8,128)(2,1)S(1)}, bf16[48,1024]{1,0:T(8,128)(2,1)S(1)}, u32[]{:S(2)}, u32[]{:S(2)}) collective-permute-start(bf16[48,1024]{1,0:T(8,128)(2,1)S(1)} %select_bitcast_fusion.23), channel_id=1, source_target_pairs={{0,16},{4,20},{8,24},{12,28},{16,0},{20,4},{24,8},{28,12},{1,17},{... | collective-permute-start | bytes 294920 | tf_op jit(solution)/shard_map/ppermute | solution.py:186
  235.7 7.2 %collective-permute-start.27 = (bf16[48,1024]{1,0:T(8,128)(2,1)S(1)}, bf16[48,1024]{1,0:T(8,128)(2,1)S(1)}, u32[]{:S(2)}, u32[]{:S(2)}) collective-permute-start(bf16[48,1024]{1,0:T(8,128)(2,1)S(1)} %select_bitcast_fusion.16), channel_id=1, source_target_pairs={{0,8},{4,12},{8,0},{12,4},{16,24},{20,28},{24,16},{28,20},{1,9},{5... | collective-permute-start | bytes 294920 | tf_op jit(solution)/shard_map/ppermute | solution.py:186
  237.8 6.8 %collective-permute-start.24 = (bf16[48,1024]{1,0:T(8,128)(2,1)S(1)}, bf16[48,1024]{1,0:T(8,128)(2,1)S(1)}, u32[]{:S(2)}, u32[]{:S(2)}) collective-permute-start(bf16[48,1024]{1,0:T(8,128)(2,1)S(1)} %select_bitcast_fusion.17), channel_id=1, source_target_pairs={{0,8},{4,12},{8,0},{12,4},{16,24},{20,28},{24,16},{28,20},{1,9},{5... | collective-permute-start | bytes 294920 | tf_op jit(solution)/shard_map/ppermute | solution.py:186
  242.9 7.8 %collective-permute-start.6 = (bf16[48,1024]{1,0:T(8,128)(2,1)S(1)}, bf16[48,1024]{1,0:T(8,128)(2,1)S(1)}, u32[]{:S(2)}, u32[]{:S(2)}) collective-permute-start(bf16[48,1024]{1,0:T(8,128)(2,1)S(1)} %get-tuple-element.16), channel_id=1, source_target_pairs={{0,1},{1,0},{2,3},{3,2},{4,5},{5,4},{6,7},{7,6},{8,9},{9,8},{10,11... | collective-permute-start | bytes 294920 | tf_op jit(solution)/shard_map/ppermute | solution.py:186
  244.7 7.1 %collective-permute-start.28 = (bf16[48,1024]{1,0:T(8,128)(2,1)S(1)}, bf16[48,1024]{1,0:T(8,128)(2,1)S(1)}, u32[]{:S(2)}, u32[]{:S(2)}) collective-permute-start(bf16[48,1024]{1,0:T(8,128)(2,1)S(1)} %get-tuple-element.28), channel_id=1, source_target_pairs={{0,1},{1,0},{2,3},{3,2},{4,5},{5,4},{6,7},{7,6},{8,9},{9,8},{10,11... | collective-permute-start | bytes 294920 | tf_op jit(solution)/shard_map/ppermute | solution.py:186
  (17 other events, 208.9 us)
